TPU v7x, 32 devices: a whole 2x2x4 slice. The times are simulated.
32 devices in a mesh: groups: 2 (over y), res: 4 (over z), col: 2 (over x), seq: 2 (over core).
Axes of the slice: x: 2, y: 2, z: 4, core: 2. Of those that a mesh axis runs over, the one named last changes fastest.
Arguments:
- alignment_states: bfloat16 [128, 128, 256], P(('groups', 'res', 'seq'), 'col'), parts along dimension 0, may hold values from -6 to 6
- standardize_scale: float32 [256], replicated, may hold values from 0.5 to 1.5
- standardize_shift: float32 [256], replicated, may hold values from -3 to 3
- first_factor_coeffs: bfloat16 [256, 32], replicated, may hold values from -0.375 to 0.375
- first_factor_offset: float32 [32], replicated, may hold values from -3 to 3
- second_factor_coeffs: bfloat16 [256, 32], replicated, may hold values from -0.375 to 0.375
- second_factor_offset: float32 [32], replicated, may hold values from -3 to 3
- final_coeffs: bfloat16 [1024, 128], replicated, may hold values from -0.1875 to 0.1875
- final_offset: float32 [128], replicated, may hold values from -3 to 3
Outputs:
- pair: bfloat16 [4, 64, 128, 128], P('groups', ('res', 'seq'), 'col'), parts along dimension 0
There are 2 independent parts, one for each index of `groups`. A program takes and returns all parts, laid end to end along the dimension named above; an argument that names none is the same for every part. Nothing has to cross between parts.
All inputs are finite; a program needn't handle non-finite values.
Results may differ from a plain program's by a relative error of at most 0.0037.
Values may be sent and summed in bfloat16 or wider, within the bound.
A program may use at most 64 MiB of HBM per device.

v0:
```python
import jax
import jax.numpy as jnp
from jax import lax
from jax.sharding import PartitionSpec as P


def project_both(rows, standardize_scale, standardize_shift, w_both, bias_both):
    input_tensor = rows.astype(jnp.float32)
    mean = jnp.mean(input_tensor, axis=-1, keepdims=True)
    centred = input_tensor - mean
    variance = jnp.mean(centred * centred, axis=-1, keepdims=True)
    normed = (centred * lax.rsqrt(variance + 1e-05) * standardize_scale + standardize_shift).astype(
        jnp.bfloat16
    )
    return (jnp.dot(normed, w_both, preferred_element_type=jnp.float32) + bias_both).astype(
        jnp.bfloat16
    )


def per_device(
    alignment_states,
    standardize_scale,
    standardize_shift,
    first_factor_coeffs,
    first_factor_offset,
    second_factor_coeffs,
    second_factor_offset,
    final_coeffs,
    final_offset,
):
    aligned_rows_each_shard, position_span, hidden_dimension = alignment_states.shape
    position_number = lax.axis_size("res")
    n_seq = lax.axis_size("seq")
    n_col = lax.axis_size("col")
    positions_each_shard = position_span // position_number
    chans = first_factor_coeffs.shape[1]
    seq_loc = aligned_rows_each_shard * position_number
    w_both = jnp.concatenate([first_factor_coeffs, second_factor_coeffs], axis=1)
    bias_both = jnp.concatenate([first_factor_offset, second_factor_offset])
    raw = lax.all_to_all(
        alignment_states.reshape(
            aligned_rows_each_shard, position_number, positions_each_shard * hidden_dimension
        ),
        "res",
        split_axis=1,
        concat_axis=0,
        tiled=True,
    )
    both = project_both(
        raw.reshape(seq_loc * positions_each_shard, hidden_dimension),
        standardize_scale,
        standardize_shift,
        w_both,
        bias_both,
    )
    both = both.reshape(seq_loc, positions_each_shard, 2 * chans)
    left_loc = both[:, :, :chans].reshape(seq_loc, positions_each_shard * chans)
    right_three = both[:, :, chans:]
    right_loc = right_three.transpose(1, 0, 2).reshape(positions_each_shard, seq_loc * chans)
    left_use = lax.all_to_all(left_loc, "seq", split_axis=1, concat_axis=0, tiled=True)
    right_use = lax.all_gather(right_loc, "seq", axis=1, tiled=True)
    rows_all = lax.all_gather(left_use, "col", axis=1, tiled=True)
    seqs = rows_all.shape[0]
    per_group = seqs // n_seq
    n_rows = rows_all.shape[1] // chans
    left_four = rows_all.reshape(n_seq, per_group, n_rows, chans)
    pair_width = final_coeffs.shape[1]
    w_deep = jnp.concatenate([final_coeffs] * n_seq, axis=0)

    def one_block(block):
        sub = block.shape[0]
        block = block.reshape(sub, n_seq, per_group, chans)
        outer = jnp.einsum("gsic,jgse->ijgce", left_four, block, preferred_element_type=jnp.float32)
        outer = outer.astype(jnp.bfloat16).reshape(n_rows * sub, n_seq * chans * chans)
        summed = jnp.dot(outer, w_deep, preferred_element_type=jnp.float32)
        return summed.reshape(n_rows, sub, pair_width)

    piece = lax.all_gather(right_use, "res", axis=0, tiled=True)
    count = piece.shape[0]
    sub = 1
    for option in range(1, 17):
        if count % option == 0:
            sub = option
    blocks = piece.reshape(count // sub, sub, piece.shape[1])
    results = lax.map(one_block, blocks)
    summed = results.transpose(1, 0, 2, 3).reshape(n_rows, count, pair_width)
    summed = summed.reshape(n_col, n_rows // n_col, summed.shape[1], pair_width)
    total = float(aligned_rows_each_shard * position_number * n_seq)
    return (summed / total + final_offset).astype(jnp.bfloat16)


def solution(mesh):
    return jax.shard_map(
        per_device,
        mesh=mesh,
        in_specs=(P(("groups", "res", "seq"), "col", None), P(), P(), P(), P(), P(), P(), P(), P()),
        out_specs=P("groups", ("res", "seq"), "col", None),
        check_vma=False,
    )
```

profile of v0, /device:TPU:0, one launch (start us, length us, event | category | flops | bytes accessed | tf_op | source)
XLA Modules:
  0.0 109.3 jit_solution(5657845986276746612)
XLA Ops:
  0.0 1.2 %reshape.58 = bf16[8,4,4096]{2,1,0:T(4,128)(2,1)S(1)} reshape(bf16[8,64,256]{2,1,0:T(8,128)(2,1)} %param.11) | data formatting | bytes 524288 | tf_op jit(solution)/shard_map/reshape | solution.py:41
  1.2 0.9 copy.21
  2.0 6.4 %all-to-all-start = ((bf16[8,4,4096]{2,0,1:T(8,128)(2,1)}), bf16[8,4,4096]{2,0,1:T(8,128)(2,1)S(1)}, u32[]{:S(2)}, u32[]{:S(2)}) async-start(bf16[8,4,4096]{2,0,1:T(8,128)(2,1)} %copy.21), calls=%async_computation | async-start | bytes 524288 | tf_op jit(solution)/shard_map/all_to_all | solution.py:40
  8.4 0.7 pad_maximum_fusion.1
  9.2 1.1 pad_maximum_fusion
  10.2 7.1 %all-to-all-done = bf16[8,4,4096]{2,0,1:T(8,128)(2,1)S(1)} async-done(((bf16[8,4,4096]{2,0,1:T(8,128)(2,1)}), bf16[8,4,4096]{2,0,1:T(8,128)(2,1)S(1)}, u32[]{:S(2)}, u32[]{:S(2)}) %all-to-all-start) | async-done | bytes 262176 | tf_op jit(solution)/shard_map/all_to_all | solution.py:40
  17.6 0.2 multiply_reduce_fusion
  17.9 0.3 fusion.4
  18.6 3.7 %all_to_all.28 = bf16[32,2,256]{2,0,1:T(8,128)(2,1)S(1)} all-to-all(bf16[32,2,256]{2,0,1:T(8,128)(2,1)S(1)} %copy.24), channel_id=1, replica_groups=mesh['groups'=2,'res'=4,'col'=2,'seq'=2] {'seq'}, dimensions={1} | all-to-all | bytes 65536 | tf_op jit(solution)/shard_map/all_to_all | solution.py:60
  22.4 4.6 %all_gather.11 = bf16[64,512]{1,0:T(8,128)(2,1)S(1)} all-gather(bf16[64,256]{1,0:T(8,128)(2,1)S(1)} %bitcast.55), channel_id=1, replica_groups=mesh['groups'=2,'res'=4,'col'=2,'seq'=2] {'col'}, dimensions={1}, use_global_device_ids=true | all-gather | bytes 98304 | tf_op jit(solution)/shard_map/all_gather | solution.py:62
  27.4 1.9 %all_gather.9 = bf16[16,2048]{1,0:T(8,128)(2,1)S(1)} all-gather(bf16[16,1024]{1,0:T(8,128)(2,1)S(1)} %reshape.60), channel_id=1, replica_groups=mesh['groups'=2,'res'=4,'col'=2,'seq'=2] {'seq'}, dimensions={1}, use_global_device_ids=true | all-gather | bytes 98304 | tf_op jit(solution)/shard_map/all_gather | solution.py:61
  29.3 13.8 %all_gather.10 = bf16[64,2048]{1,0:T(8,128)(2,1)S(1)} all-gather(bf16[16,2048]{1,0:T(8,128)(2,1)S(1)} %all_gather.9), channel_id=1, replica_groups=mesh['groups'=2,'res'=4,'col'=2,'seq'=2] {'res'}, dimensions={0}, use_global_device_ids=true | all-gather | bytes 327680 | tf_op jit(solution)/shard_map/all_gather | solution.py:78
  43.1 65.3 %while.10 = (s32[]{:T(128)}, f32[4,16,16,128]{3,2,1,0:T(8,128)S(1)}, bf16[4,16,2048]{2,1,0:T(8,128)(2,1)S(1)}, bf16[2,32,16,32]{3,1,2,0:T(8,128)(2,1)S(1)}, bf16[2048,128]{1,0:T(8,128)(2,1)S(1)}, /*index=5*/s32[]{:T(128)}) while((s32[]{:T(128)}, f32[4,16,16,128]{3,2,1,0:T(8,128)S(1)}, bf16[4,16,2048]{2,1,0:T(8,128)(2,1)S(1)}, ...), condition=%wide.region_3.4_spmd, body=%wide.region_2.3_spmd.sunk | while | flops 168296448 | bytes 7340109 | solution.py:85
  43.1 0.2 reshape.70
  43.3 3.2 %convert_bitcast_fusion.3 = bf16[16,16,2,32,32]{3,4,0,1,2:T(8,128)(2,1)} fusion(bf16[2,32,16,32]{3,1,2,0:T(8,128)(2,1)S(1)} %get-tuple-element.101, bf16[16,2,32,32]{3,2,1,0:T(8,128)(2,1)S(1)} %reshape.70), kind=kOutput, calls=%fused_computation.clone.1 | convolution fusion | flops 34078720 | bytes 1179648 | tf_op jit(solution)/shard_map/while/body/eval_jaxpr/gsic,jgse->ijgce/dot_general | solution.py:73
  46.5 6.4 %copy.36 = bf16[16,16,2,32,32]{4,3,2,1,0:T(8,128)(2,1)} copy(bf16[16,16,2,32,32]{3,4,0,1,2:T(8,128)(2,1)} %convert_bitcast_fusion.3) | data formatting | bytes 2097152 | tf_op jit(solution)/shard_map/while/body/eval_jaxpr/convert_element_type | solution.py:74
  53.0 6.0 %reshape.71 = bf16[16,16,2048]{2,1,0:T(8,128)(2,1)S(1)} reshape(bf16[16,16,2,32,32]{4,3,2,1,0:T(8,128)(2,1)} %copy.36) | data formatting | bytes 2097152 | tf_op jit(solution)/shard_map/reshape.23
  59.0 0.4 fusion.27
  59.4 0.2 reshape.70
  59.6 3.2 %convert_bitcast_fusion.3 = bf16[16,16,2,32,32]{3,4,0,1,2:T(8,128)(2,1)} fusion(bf16[2,32,16,32]{3,1,2,0:T(8,128)(2,1)S(1)} %get-tuple-element.101, bf16[16,2,32,32]{3,2,1,0:T(8,128)(2,1)S(1)} %reshape.70), kind=kOutput, calls=%fused_computation.clone.1 | convolution fusion | flops 34078720 | bytes 1179648 | tf_op jit(solution)/shard_map/while/body/eval_jaxpr/gsic,jgse->ijgce/dot_general | solution.py:73
  62.9 6.4 %copy.36 = bf16[16,16,2,32,32]{4,3,2,1,0:T(8,128)(2,1)} copy(bf16[16,16,2,32,32]{3,4,0,1,2:T(8,128)(2,1)} %convert_bitcast_fusion.3) | data formatting | bytes 2097152 | tf_op jit(solution)/shard_map/while/body/eval_jaxpr/convert_element_type | solution.py:74
  69.3 6.0 %reshape.71 = bf16[16,16,2048]{2,1,0:T(8,128)(2,1)S(1)} reshape(bf16[16,16,2,32,32]{4,3,2,1,0:T(8,128)(2,1)} %copy.36) | data formatting | bytes 2097152 | tf_op jit(solution)/shard_map/reshape.23
  75.3 0.4 fusion.27
  76.0 3.2 %convert_bitcast_fusion.3 = bf16[16,16,2,32,32]{3,4,0,1,2:T(8,128)(2,1)} fusion(bf16[2,32,16,32]{3,1,2,0:T(8,128)(2,1)S(1)} %get-tuple-element.101, bf16[16,2,32,32]{3,2,1,0:T(8,128)(2,1)S(1)} %reshape.70), kind=kOutput, calls=%fused_computation.clone.1 | convolution fusion | flops 34078720 | bytes 1179648 | tf_op jit(solution)/shard_map/while/body/eval_jaxpr/gsic,jgse->ijgce/dot_general | solution.py:73
  79.2 6.4 %copy.36 = bf16[16,16,2,32,32]{4,3,2,1,0:T(8,128)(2,1)} copy(bf16[16,16,2,32,32]{3,4,0,1,2:T(8,128)(2,1)} %convert_bitcast_fusion.3) | data formatting | bytes 2097152 | tf_op jit(solution)/shard_map/while/body/eval_jaxpr/convert_element_type | solution.py:74
  85.6 6.0 %reshape.71 = bf16[16,16,2048]{2,1,0:T(8,128)(2,1)S(1)} reshape(bf16[16,16,2,32,32]{4,3,2,1,0:T(8,128)(2,1)} %copy.36) | data formatting | bytes 2097152 | tf_op jit(solution)/shard_map/reshape.23
  91.6 0.4 fusion.27
  92.3 3.2 %convert_bitcast_fusion.3 = bf16[16,16,2,32,32]{3,4,0,1,2:T(8,128)(2,1)} fusion(bf16[2,32,16,32]{3,1,2,0:T(8,128)(2,1)S(1)} %get-tuple-element.101, bf16[16,2,32,32]{3,2,1,0:T(8,128)(2,1)S(1)} %reshape.70), kind=kOutput, calls=%fused_computation.clone.1 | convolution fusion | flops 34078720 | bytes 1179648 | tf_op jit(solution)/shard_map/while/body/eval_jaxpr/gsic,jgse->ijgce/dot_general | solution.py:73
  95.5 6.4 %copy.36 = bf16[16,16,2,32,32]{4,3,2,1,0:T(8,128)(2,1)} copy(bf16[16,16,2,32,32]{3,4,0,1,2:T(8,128)(2,1)} %convert_bitcast_fusion.3) | data formatting | bytes 2097152 | tf_op jit(solution)/shard_map/while/body/eval_jaxpr/convert_element_type | solution.py:74
  102.0 6.0 %reshape.71 = bf16[16,16,2048]{2,1,0:T(8,128)(2,1)S(1)} reshape(bf16[16,16,2,32,32]{4,3,2,1,0:T(8,128)(2,1)} %copy.36) | data formatting | bytes 2097152 | tf_op jit(solution)/shard_map/reshape.23
  108.0 0.4 fusion.27
  108.5 0.8 add_convert_fusion
  (32 shorter events, 1.6 us)
Async XLA Ops:
  0.0 17.9 %copy-start.4 = (f32[256]{0:T(256)S(1)}, f32[256]{0:T(256)}, u32[]{:S(2)}) copy-start(f32[256]{0:T(256)} %param.12) | copy-start | bytes 3076
  0.0 17.9 %copy-start.3 = (f32[256]{0:T(256)S(1)}, f32[256]{0:T(256)}, u32[]{:S(2)}) copy-start(f32[256]{0:T(256)} %param.13) | copy-start | bytes 3076
  0.0 17.9 %copy-start.2 = (bf16[256,32]{0,1:T(8,128)(2,1)S(1)}, bf16[256,32]{0,1:T(8,128)(2,1)}, u32[]{:S(2)}) copy-start(bf16[256,32]{0,1:T(8,128)(2,1)} %param.14) | copy-start | bytes 49156
  0.0 17.9 %copy-start.1 = (bf16[256,32]{0,1:T(8,128)(2,1)S(1)}, bf16[256,32]{0,1:T(8,128)(2,1)}, u32[]{:S(2)}) copy-start(bf16[256,32]{0,1:T(8,128)(2,1)} %param.16) | copy-start | bytes 49156
  2.0 15.3 %all-to-all-start = ((bf16[8,4,4096]{2,0,1:T(8,128)(2,1)}), bf16[8,4,4096]{2,0,1:T(8,128)(2,1)S(1)}, u32[]{:S(2)}, u32[]{:S(2)}) async-start(bf16[8,4,4096]{2,0,1:T(8,128)(2,1)} %copy.21), calls=%async_computation | async-start | bytes 524288 | tf_op jit(solution)/shard_map/all_to_all | solution.py:40
  43.1 65.4 %copy-start = (f32[128]{0:T(128)S(1)}, f32[128]{0:T(128)}, u32[]{:S(2)}) copy-start(f32[128]{0:T(128)} %param.19) | copy-start | bytes 1540
where the time goes:
time: 110 us; the launch traced here: 109 us
  local copies, waits for them, and re-layouts  53.6 us (49%)
  blocking collectives  24 us (22%)
  matrix products  15 us (14%)
  waiting for transfers between devices  7.1 us (6%)
  starting transfers between devices  6.36 us (6%)
  other arithmetic  3.04 us (3%)
    convert_element_type x4, local copies, waits for them, and re-layouts, one_block(): outer.astype(jnp.bfloat16).reshape(n_rows * sub, n_seq * chans * chans)  25.8 us
    another operation x4, local copies, waits for them, and re-layouts  24 us
    all_gather x1, blocking collectives, per_device(): piece = lax.all_gather(right_use, 'res', axis=0, tiled=True)  13.8 us
    dot_general x4, matrix products, one_block(): jnp.einsum('gsic,jgse->ijgce', left_four, block, preferred_element_type=j...  12.9 us
    all_to_all x1, waiting for transfers between devices, per_device(): lax.all_to_all(alignment_states.reshape(aligned_rows_each_shard, position...  7.1 us
    all_to_all x1, starting transfers between devices, per_device(): lax.all_to_all(alignment_states.reshape(aligned_rows_each_shard, position...  6.36 us
    all_gather x1, blocking collectives, per_device(): rows_all = lax.all_gather(left_use, 'col', axis=1, tiled=True)  4.57 us
    all_to_all x1, blocking collectives, per_device(): lax.all_to_all(left_loc, 'seq', split_axis=1, concat_axis=0, tiled=True)  3.75 us
  transfers between devices with their start and end apart: 1, of which 1 were waited for; matrix products, arithmetic and copies ran while one was open for 2% of the time, Pallas kernels for 0%

commit v1 on v0

--- a/solution.py
+++ b/solution.py
@@ -37,14 +37,24 @@
     seq_loc = aligned_rows_each_shard * position_number
     w_both = jnp.concatenate([first_factor_coeffs, second_factor_coeffs], axis=1)
     bias_both = jnp.concatenate([first_factor_offset, second_factor_offset])
-    raw = lax.all_to_all(
-        alignment_states.reshape(
-            aligned_rows_each_shard, position_number, positions_each_shard * hidden_dimension
+    raw = jnp.concatenate(
+        lax.all_to_all(
+            jnp.stack(
+                jnp.split(
+                    alignment_states.reshape(
+                        aligned_rows_each_shard,
+                        position_number,
+                        positions_each_shard * hidden_dimension,
+                    ),
+                    lax.axis_size("res"),
+                    axis=1,
+                )
+            ),
+            "res",
+            0,
+            0,
         ),
-        "res",
-        split_axis=1,
-        concat_axis=0,
-        tiled=True,
+        axis=0,
     )
     both = project_both(
         raw.reshape(seq_loc * positions_each_shard, hidden_dimension),

time: 110 us -> 111 us (level)
  no operation moved by 1% of the time
where the time goes in v1:
time: 111 us; the launch traced here: 110 us
  local copies, waits for them, and re-layouts  53.6 us (48%)
  blocking collectives  24 us (22%)
  matrix products  15 us (14%)
  waiting for transfers between devices  7.1 us (6%)
  starting transfers between devices  6.36 us (6%)
  other arithmetic  3.74 us (3%)
    convert_element_type x4, local copies, waits for them, and re-layouts, one_block(): outer.astype(jnp.bfloat16).reshape(n_rows * sub, n_seq * chans * chans)  25.8 us
    another operation x4, local copies, waits for them, and re-layouts  24 us
    all_gather x1, blocking collectives, per_device(): piece = lax.all_gather(right_use, 'res', axis=0, tiled=True)  13.8 us
    dot_general x4, matrix products, one_block(): jnp.einsum('gsic,jgse->ijgce', left_four, block, preferred_element_type=j...  12.9 us
    all_to_all x1, waiting for transfers between devices, per_device(): lax.all_to_all(jnp.stack(jnp.split(alignment_states.reshape(aligned_rows_...  7.1 us
    all_to_all x1, starting transfers between devices, per_device(): lax.all_to_all(jnp.stack(jnp.split(alignment_states.reshape(aligned_rows_...  6.36 us
    all_gather x1, blocking collectives, per_device(): rows_all = lax.all_gather(left_use, 'col', axis=1, tiled=True)  4.57 us
    all_to_all x1, blocking collectives, per_device(): lax.all_to_all(left_loc, 'seq', split_axis=1, concat_axis=0, tiled=True)  3.75 us
  transfers between devices with their start and end apart: 1, of which 1 were waited for; matrix products, arithmetic and copies ran while one was open for 2% of the time, Pallas kernels for 0%

profile of v1, /device:TPU:0, one launch (start us, length us, event | category | flops | bytes accessed | tf_op | source)
XLA Modules:
  0.0 110.1 jit_solution(8696647036796812555)
XLA Ops:
  0.0 1.2 %reshape.54 = bf16[8,4,4096]{2,1,0:T(4,128)(2,1)S(1)} reshape(bf16[8,64,256]{2,1,0:T(8,128)(2,1)} %param.11) | data formatting | bytes 524288 | tf_op jit(solution)/shard_map/reshape | solution.py:44
  1.2 0.5 fusion.13
  2.1 0.7 pad_maximum_fusion.1
  2.8 6.4 %all-to-all-start = ((bf16[4,8,1,4096]{3,1,2,0:T(8,128)(2,1)}), bf16[4,8,1,4096]{3,1,2,0:T(8,128)(2,1)S(1)}, u32[]{:S(2)}, u32[]{:S(2)}) async-start(bf16[4,8,1,4096]{3,1,2,0:T(8,128)(2,1)} %pad_maximum_fusion.1), calls=%async_computation | async-start | bytes 524288 | tf_op jit(solution)/shard_map/all_to_all | solution.py:41
  9.2 0.7 pad_maximum_fusion.2
  9.9 1.1 pad_maximum_fusion
  11.0 7.1 %all-to-all-done = bf16[4,8,1,4096]{3,1,2,0:T(8,128)(2,1)S(1)} async-done(((bf16[4,8,1,4096]{3,1,2,0:T(8,128)(2,1)}), bf16[4,8,1,4096]{3,1,2,0:T(8,128)(2,1)S(1)}, u32[]{:S(2)}, u32[]{:S(2)}) %all-to-all-start) | async-done | bytes 262176 | tf_op jit(solution)/shard_map/all_to_all | solution.py:41
  18.3 0.2 multiply_reduce_fusion
  18.6 0.3 fusion.4
  19.4 3.7 %all_to_all.24 = bf16[32,2,256]{2,0,1:T(8,128)(2,1)S(1)} all-to-all(bf16[32,2,256]{2,0,1:T(8,128)(2,1)S(1)} %copy.56), channel_id=1, replica_groups=mesh['groups'=2,'res'=4,'col'=2,'seq'=2] {'seq'}, dimensions={1} | all-to-all | bytes 65536 | tf_op jit(solution)/shard_map/all_to_all | solution.py:70
  23.1 4.6 %all_gather.11 = bf16[64,512]{1,0:T(8,128)(2,1)S(1)} all-gather(bf16[64,256]{1,0:T(8,128)(2,1)S(1)} %bitcast.58), channel_id=1, replica_groups=mesh['groups'=2,'res'=4,'col'=2,'seq'=2] {'col'}, dimensions={1}, use_global_device_ids=true | all-gather | bytes 98304 | tf_op jit(solution)/shard_map/all_gather | solution.py:72
  28.2 1.9 %all_gather.9 = bf16[16,2048]{1,0:T(8,128)(2,1)S(1)} all-gather(bf16[16,1024]{1,0:T(8,128)(2,1)S(1)} %reshape.56), channel_id=1, replica_groups=mesh['groups'=2,'res'=4,'col'=2,'seq'=2] {'seq'}, dimensions={1}, use_global_device_ids=true | all-gather | bytes 98304 | tf_op jit(solution)/shard_map/all_gather | solution.py:71
  30.0 13.8 %all_gather.10 = bf16[64,2048]{1,0:T(8,128)(2,1)S(1)} all-gather(bf16[16,2048]{1,0:T(8,128)(2,1)S(1)} %all_gather.9), channel_id=1, replica_groups=mesh['groups'=2,'res'=4,'col'=2,'seq'=2] {'res'}, dimensions={0}, use_global_device_ids=true | all-gather | bytes 327680 | tf_op jit(solution)/shard_map/all_gather | solution.py:88
  43.8 65.4 %while.10 = (s32[]{:T(128)}, f32[4,16,16,128]{3,2,1,0:T(8,128)S(1)}, bf16[4,16,2048]{2,1,0:T(8,128)(2,1)S(1)}, bf16[2,32,16,32]{3,1,2,0:T(8,128)(2,1)S(1)}, bf16[2048,128]{1,0:T(8,128)(2,1)S(1)}, /*index=5*/s32[]{:T(128)}) while((s32[]{:T(128)}, f32[4,16,16,128]{3,2,1,0:T(8,128)S(1)}, bf16[4,16,2048]{2,1,0:T(8,128)(2,1)S(1)}, ...), condition=%wide.region_3.4_spmd, body=%wide.region_2.3_spmd.sunk | while | flops 168296448 | bytes 7340109 | solution.py:95
  43.8 0.2 reshape.65
  44.0 3.2 %convert_bitcast_fusion.2 = bf16[16,16,2,32,32]{3,4,0,1,2:T(8,128)(2,1)} fusion(bf16[2,32,16,32]{3,1,2,0:T(8,128)(2,1)S(1)} %get-tuple-element.129, bf16[16,2,32,32]{3,2,1,0:T(8,128)(2,1)S(1)} %reshape.65), kind=kOutput, calls=%fused_computation.clone.1 | convolution fusion | flops 34078720 | bytes 1179648 | tf_op jit(solution)/shard_map/while/body/eval_jaxpr/gsic,jgse->ijgce/dot_general | solution.py:83
  47.3 6.5 %copy.76 = bf16[16,16,2,32,32]{4,3,2,1,0:T(8,128)(2,1)} copy(bf16[16,16,2,32,32]{3,4,0,1,2:T(8,128)(2,1)} %convert_bitcast_fusion.2) | data formatting | bytes 2097152 | tf_op jit(solution)/shard_map/while/body/eval_jaxpr/convert_element_type | solution.py:84
  53.7 6.0 %reshape.66 = bf16[16,16,2048]{2,1,0:T(8,128)(2,1)S(1)} reshape(bf16[16,16,2,32,32]{4,3,2,1,0:T(8,128)(2,1)} %copy.76) | data formatting | bytes 2097152 | tf_op jit(solution)/shard_map/reshape.21
  59.7 0.4 fusion.28
  60.4 3.2 %convert_bitcast_fusion.2 = bf16[16,16,2,32,32]{3,4,0,1,2:T(8,128)(2,1)} fusion(bf16[2,32,16,32]{3,1,2,0:T(8,128)(2,1)S(1)} %get-tuple-element.129, bf16[16,2,32,32]{3,2,1,0:T(8,128)(2,1)S(1)} %reshape.65), kind=kOutput, calls=%fused_computation.clone.1 | convolution fusion | flops 34078720 | bytes 1179648 | tf_op jit(solution)/shard_map/while/body/eval_jaxpr/gsic,jgse->ijgce/dot_general | solution.py:83
  63.6 6.5 %copy.76 = bf16[16,16,2,32,32]{4,3,2,1,0:T(8,128)(2,1)} copy(bf16[16,16,2,32,32]{3,4,0,1,2:T(8,128)(2,1)} %convert_bitcast_fusion.2) | data formatting | bytes 2097152 | tf_op jit(solution)/shard_map/while/body/eval_jaxpr/convert_element_type | solution.py:84
  70.1 6.0 %reshape.66 = bf16[16,16,2048]{2,1,0:T(8,128)(2,1)S(1)} reshape(bf16[16,16,2,32,32]{4,3,2,1,0:T(8,128)(2,1)} %copy.76) | data formatting | bytes 2097152 | tf_op jit(solution)/shard_map/reshape.21
  76.1 0.4 fusion.28
  76.7 3.2 %convert_bitcast_fusion.2 = bf16[16,16,2,32,32]{3,4,0,1,2:T(8,128)(2,1)} fusion(bf16[2,32,16,32]{3,1,2,0:T(8,128)(2,1)S(1)} %get-tuple-element.129, bf16[16,2,32,32]{3,2,1,0:T(8,128)(2,1)S(1)} %reshape.65), kind=kOutput, calls=%fused_computation.clone.1 | convolution fusion | flops 34078720 | bytes 1179648 | tf_op jit(solution)/shard_map/while/body/eval_jaxpr/gsic,jgse->ijgce/dot_general | solution.py:83
  80.0 6.5 %copy.76 = bf16[16,16,2,32,32]{4,3,2,1,0:T(8,128)(2,1)} copy(bf16[16,16,2,32,32]{3,4,0,1,2:T(8,128)(2,1)} %convert_bitcast_fusion.2) | data formatting | bytes 2097152 | tf_op jit(solution)/shard_map/while/body/eval_jaxpr/convert_element_type | solution.py:84
  86.4 6.0 %reshape.66 = bf16[16,16,2048]{2,1,0:T(8,128)(2,1)S(1)} reshape(bf16[16,16,2,32,32]{4,3,2,1,0:T(8,128)(2,1)} %copy.76) | data formatting | bytes 2097152 | tf_op jit(solution)/shard_map/reshape.21
  92.4 0.4 fusion.28
  93.1 3.2 %convert_bitcast_fusion.2 = bf16[16,16,2,32,32]{3,4,0,1,2:T(8,128)(2,1)} fusion(bf16[2,32,16,32]{3,1,2,0:T(8,128)(2,1)S(1)} %get-tuple-element.129, bf16[16,2,32,32]{3,2,1,0:T(8,128)(2,1)S(1)} %reshape.65), kind=kOutput, calls=%fused_computation.clone.1 | convolution fusion | flops 34078720 | bytes 1179648 | tf_op jit(solution)/shard_map/while/body/eval_jaxpr/gsic,jgse->ijgce/dot_general | solution.py:83
  96.3 6.5 %copy.76 = bf16[16,16,2,32,32]{4,3,2,1,0:T(8,128)(2,1)} copy(bf16[16,16,2,32,32]{3,4,0,1,2:T(8,128)(2,1)} %convert_bitcast_fusion.2) | data formatting | bytes 2097152 | tf_op jit(solution)/shard_map/while/body/eval_jaxpr/convert_element_type | solution.py:84
  102.7 6.0 %reshape.66 = bf16[16,16,2048]{2,1,0:T(8,128)(2,1)S(1)} reshape(bf16[16,16,2,32,32]{4,3,2,1,0:T(8,128)(2,1)} %copy.76) | data formatting | bytes 2097152 | tf_op jit(solution)/shard_map/reshape.21
  108.8 0.4 fusion.28
  109.3 0.8 add_convert_fusion
  (34 shorter events, 2.1 us)
Async XLA Ops:
  0.0 18.6 %copy-start.4 = (f32[256]{0:T(256)S(1)}, f32[256]{0:T(256)}, u32[]{:S(2)}) copy-start(f32[256]{0:T(256)} %param.12) | copy-start | bytes 3076
  0.0 18.6 %copy-start.3 = (f32[256]{0:T(256)S(1)}, f32[256]{0:T(256)}, u32[]{:S(2)}) copy-start(f32[256]{0:T(256)} %param.13) | copy-start | bytes 3076
  0.0 18.6 %copy-start.2 = (bf16[256,32]{0,1:T(8,128)(2,1)S(1)}, bf16[256,32]{0,1:T(8,128)(2,1)}, u32[]{:S(2)}) copy-start(bf16[256,32]{0,1:T(8,128)(2,1)} %param.14) | copy-start | bytes 49156
  0.0 18.6 %copy-start.1 = (bf16[256,32]{0,1:T(8,128)(2,1)S(1)}, bf16[256,32]{0,1:T(8,128)(2,1)}, u32[]{:S(2)}) copy-start(bf16[256,32]{0,1:T(8,128)(2,1)} %param.16) | copy-start | bytes 49156
  2.8 15.3 %all-to-all-start = ((bf16[4,8,1,4096]{3,1,2,0:T(8,128)(2,1)}), bf16[4,8,1,4096]{3,1,2,0:T(8,128)(2,1)S(1)}, u32[]{:S(2)}, u32[]{:S(2)}) async-start(bf16[4,8,1,4096]{3,1,2,0:T(8,128)(2,1)} %pad_maximum_fusion.1), calls=%async_computation | async-start | bytes 524288 | tf_op jit(solution)/shard_map/all_to_all | solution.py:41
  43.8 65.5 %copy-start = (f32[128]{0:T(128)S(1)}, f32[128]{0:T(128)}, u32[]{:S(2)}) copy-start(f32[128]{0:T(128)} %param.19) | copy-start | bytes 1540
